TPU v7x, 32 devices: a whole 2x2x4 slice. The times are simulated.
32 devices in a mesh: section: 4 (over x, core), dp: 8 (over z, y).
Axes of the slice: x: 2, y: 2, z: 4, core: 2. Of those that a mesh axis runs over, the one named last changes fastest.
Arguments:
- token_ids: int32 [2, 16], P(None, 'dp'), may hold values from 0 to 8191
- target_ids: int32 [2, 16], P(None, 'dp'), may hold values from 0 to 8191
- table: bfloat16 [8192, 4608], P(('section', 'dp')), may hold values from -0.06629126 to 0.06629126
- norm_gain: bfloat16 [2, 4, 4608], P(None, 'section'), may hold values from 0.099609375 to 1.8984375
- w_in: bfloat16 [2, 4, 8, 4608], P(None, 'section'), may hold values from -0.09375 to 0.09375
- w_out: bfloat16 [2, 4, 8, 4608], P(None, 'section'), may hold values from -2 to 2
- final_gain: bfloat16 [4608], replicated, may hold values from 0.099609375 to 1.8984375
Outputs:
- token_loss: float32 [2, 16], P(None, 'dp')
- table_grad: bfloat16 [8192, 4608], P(('section', 'dp'))
All inputs are finite; a program needn't handle non-finite values.
Results may differ from a plain program's by a relative error of at most 0.013.
The roundings to bfloat16 on the way count: a program that leaves them out, or rounds other values in their place, can miss the bound.
Values may be sent and summed in bfloat16 or wider, within the bound.
A program may use at most 64 MiB of HBM per device.

v0:
```python
import math
import jax
import jax.numpy as jnp
from jax import lax
from jax.sharding import PartitionSpec as P

EPS = 1e-06
CAP = 30.0
GELU_C = 0.7978845608028654


def shifted(block, axis, distance):
    devices = range(lax.axis_size(axis))
    route = [((i - distance) % len(devices), i) for i in devices]
    return lax.ppermute(block, axis, route)


def from_root(block, axis, source):
    block = jnp.where(lax.axis_index(axis) == source, block, jnp.zeros_like(block))
    return lax.psum(block, axis)


def gelu_tanh(values):
    return 0.5 * values * (1.0 + jnp.tanh(GELU_C * (values + 0.044715 * values * values * values)))


def gelu_slope(values):
    inner = jnp.tanh(GELU_C * (values + 0.044715 * values * values * values))
    return 0.5 * (1.0 + inner) + 0.5 * values * (1.0 - inner * inner) * GELU_C * (
        1.0 + 3.0 * 0.044715 * values * values
    )


def normalize(rows_in):
    values = rows_in.astype(jnp.float32)
    scale = lax.rsqrt(jnp.mean(values * values, axis=-1, keepdims=True) + EPS)
    return (values * scale, scale)


def norm_back(normed, scale, grad):
    return scale * (grad - normed * jnp.mean(grad * normed, axis=-1, keepdims=True))


def layer_forward(rows_in, gain, first_proj, second_proj):
    normed, scale = normalize(rows_in)
    activated = (normed * gain.astype(jnp.float32)).astype(jnp.bfloat16)
    preact = lax.dot_general(
        activated, first_proj, (((1,), (1,)), ((), ())), preferred_element_type=jnp.float32
    )
    hidden = gelu_tanh(preact).astype(jnp.bfloat16)
    branch = jnp.dot(hidden, second_proj, preferred_element_type=jnp.float32)
    return (rows_in.astype(jnp.float32) + branch).astype(jnp.bfloat16)


def layer_backward(rows_in, gain, first_proj, second_proj, grad_out):
    normed, scale = normalize(rows_in)
    gain_float = gain.astype(jnp.float32)
    activated = (normed * gain_float).astype(jnp.bfloat16)
    preact = lax.dot_general(
        activated, first_proj, (((1,), (1,)), ((), ())), preferred_element_type=jnp.float32
    )
    hidden_grad = lax.dot_general(
        grad_out, second_proj, (((1,), (1,)), ((), ())), preferred_element_type=jnp.float32
    )
    preact_grad = (hidden_grad * gelu_slope(preact)).astype(jnp.bfloat16)
    act_grad = jnp.dot(preact_grad, first_proj, preferred_element_type=jnp.float32)
    return (grad_out.astype(jnp.float32) + norm_back(normed, scale, act_grad * gain_float)).astype(
        jnp.bfloat16
    )


def per_device(token_ids, target_ids, table, norm_gain, w_in, w_out, final_gain):
    sections = lax.axis_size("section")
    section_index = lax.axis_index("section")
    replicas = lax.axis_size("dp")
    replica_index = lax.axis_index("dp")
    batches, width = token_ids.shape
    rows_dev, dim = table.shape
    embed_scale = math.sqrt(dim)
    offset = (section_index * replicas + replica_index) * rows_dev
    columns = jnp.arange(rows_dev, dtype=jnp.int32)
    final_scale = final_gain.astype(jnp.float32)
    ids = lax.all_gather(jnp.concatenate([token_ids, target_ids], 0), "dp", axis=1, tiled=True)
    gains = lax.all_gather(norm_gain, "section", axis=1, tiled=True).reshape(-1, dim)
    first = lax.all_gather(w_in, "section", axis=1, tiled=True).reshape(2 * sections, -1, dim)
    second = lax.all_gather(w_out, "section", axis=1, tiled=True).reshape(2 * sections, -1, dim)
    all_inputs, all_targets = (ids[:batches], ids[batches:])
    wide = all_inputs.shape[1]
    token_count = batches * wide
    chosen = ((all_inputs.reshape(token_count) - offset)[:, None] == columns[None, :]).astype(
        jnp.bfloat16
    )
    looked = jnp.dot(chosen, table, preferred_element_type=jnp.float32).astype(jnp.bfloat16)
    looked = lax.psum(looked, ("section", "dp")).astype(jnp.float32)
    rows = (looked * embed_scale).astype(jnp.bfloat16)

    def forward(rows, weights):
        return (layer_forward(rows, *weights), rows)

    rows, inputs = lax.scan(forward, rows, (gains, first, second))
    normed, scale = normalize(rows)
    head_input = (normed * final_scale).astype(jnp.bfloat16)
    scores = lax.dot_general(
        head_input, table, (((1,), (1,)), ((), ())), preferred_element_type=jnp.float32
    )
    squash = jnp.tanh(scores / CAP)
    capped = CAP * squash
    powers = jnp.exp(capped)
    goal_local = all_targets.reshape(token_count) - offset
    target_mask = goal_local[:, None] == columns[None, :]
    stats = lax.psum(
        jnp.stack(
            [
                jnp.sum(powers, axis=1),
                jnp.sum(jnp.where(target_mask, capped, jnp.float32(0.0)), axis=1),
            ]
        ),
        ("section", "dp"),
    )
    exp_total, target_score = (stats[0], stats[1])
    loss_all = (jnp.log(exp_total) - target_score).reshape(batches, wide)
    token_loss = lax.dynamic_slice_in_dim(loss_all, replica_index * width, width, 1)
    score_grad = (
        (powers / exp_total[:, None] - target_mask.astype(jnp.float32)) * (1.0 - squash * squash)
    ).astype(jnp.bfloat16)
    partial_value = jnp.dot(score_grad, table, preferred_element_type=jnp.float32)
    head_in_grad = lax.psum(partial_value, ("section", "dp"))
    grad = norm_back(normed, scale, head_in_grad * final_scale).astype(jnp.bfloat16)

    def backward(grad, saved):
        return (layer_backward(*saved, grad), None)

    grad, _ = lax.scan(backward, grad, (inputs, gains, first, second), reverse=True)
    head_grad = lax.dot_general(
        score_grad, head_input, (((0,), (0,)), ((), ())), preferred_element_type=jnp.float32
    )
    embed_grad = (
        lax.dot_general(chosen, grad, (((0,), (0,)), ((), ())), preferred_element_type=jnp.float32)
        * embed_scale
    )
    return (token_loss, (head_grad + embed_grad).astype(jnp.bfloat16))


def solution(mesh):
    return jax.shard_map(
        per_device,
        mesh=mesh,
        in_specs=(
            P(None, "dp"),
            P(None, "dp"),
            P(("section", "dp"), None),
            P(None, "section", None),
            P(None, "section", None, None),
            P(None, "section", None, None),
            P(),
        ),
        out_specs=(P(None, "dp"), P(("section", "dp"), None)),
        check_vma=False,
    )
```

profile of v0, /device:TPU:0, one launch (start us, length us, event | category | flops | bytes accessed | tf_op | source)
XLA Modules:
  0.0 419.9 jit_solution(2897440791546498494)
XLA Ops:
  8.2 22.3 %all-gather = s32[8,2,4]{2,1,0:T(2,128)S(1)} all-gather(s32[1,2,4]{2,1,0:T(2,128)S(1)} %bitcast.102), channel_id=1, replica_groups=mesh['section'=4,'dp'=8] {'dp'}, dimensions={0}, use_global_device_ids=true | all-gather | bytes 288 | tf_op jit(solution)/shard_map/all_gather | solution.py:83
  30.6 1.2 convolution_convert_fusion
  32.1 5.3 %all_gather.13 = bf16[2,4,4608]{2,0,1:T(2,128)(2,1)S(1)} all-gather(bf16[2,1,4608]{2,0,1:T(2,128)(2,1)S(1)} %copy-done.3), channel_id=1, replica_groups=mesh['section'=4,'dp'=8] {'section'}, dimensions={1}, use_global_device_ids=true | all-gather | bytes 92160 | tf_op jit(solution)/shard_map/all_gather | solution.py:84
  38.0 8.2 %all_gather.14 = bf16[2,4,8,4608]{3,2,1,0:T(8,128)(2,1)} all-gather(bf16[2,1,8,4608]{3,2,1,0:T(8,128)(2,1)S(1)} %copy-done.1), channel_id=1, replica_groups=mesh['section'=4,'dp'=8] {'section'}, dimensions={1}, use_global_device_ids=true | all-gather | bytes 737280 | tf_op jit(solution)/shard_map/all_gather | solution.py:85
  46.2 8.1 %all_gather.15 = bf16[2,4,8,4608]{3,2,1,0:T(8,128)(2,1)} all-gather(bf16[2,1,8,4608]{3,2,1,0:T(8,128)(2,1)S(1)} %copy-done.2), channel_id=1, replica_groups=mesh['section'=4,'dp'=8] {'section'}, dimensions={1}, use_global_device_ids=true | all-gather | bytes 737280 | tf_op jit(solution)/shard_map/all_gather | solution.py:86
  54.3 100.7 %all-reduce.3.cloned.1.call-done = bf16[32,4608]{1,0:T(8,128)(2,1)} async-done(((bf16[32,4608]{1,0:T(8,128)(2,1)}), bf16[32,4608]{1,0:T(8,128)(2,1)}) %all-reduce.3.cloned.1.call-update) | async-done | bytes 294928 | tf_op jit(solution)/shard_map/psum | solution.py:94
  156.0 28.2 %while.26 = (s32[]{:T(128)}, bf16[32,4608]{1,0:T(8,128)(2,1)S(1)}, bf16[8,32,4608]{2,1,0:T(8,128)(2,1)}, bf16[8,4608]{1,0:T(8,128)(2,1)}, bf16[8,8,4608]{2,1,0:T...) while((s32[]{:T(128)}, bf16[32,4608]{1,0:T(8,128)(2,1)S(1)}, bf16[8,32,4608]{2,1,0:T(8,128)(2,1)}, ...), condition=%wide.region_3.4_spmd, body=%wide.region_1.3_spmd.sunk | while | flops 6200098 | bytes 2556893 | solution.py:100
  157.9 1.6 fusion.132
  161.5 1.6 fusion.132
  165.0 1.6 fusion.132
  168.5 1.6 fusion.132
  172.1 1.6 fusion.132
  175.6 1.6 fusion.132
  179.1 1.6 fusion.132
  182.7 1.6 fusion.132
  185.4 41.2 %psum.22 = f32[2,32]{1,0:T(2,128)S(1)} all-reduce(f32[2,32]{1,0:T(2,128)S(1)} %pad_maximum_fusion), channel_id=1, replica_groups=mesh['section'=4,'dp'=8] {'section','dp'}, use_global_device_ids=true, to_apply=%region_7.8 | all-reduce | flops 64 | bytes 512 | tf_op jit(solution)/shard_map/psum | solution.py:111
  226.7 1.4 fusion.107
  228.8 3.0 fusion.102
  231.8 123.7 %all-reduce.5.cloned.1.call-done = f32[32,4608]{1,0:T(8,128)} async-done(((f32[32,4608]{1,0:T(8,128)}), f32[32,4608]{1,0:T(8,128)}) %all-reduce.5.cloned.1.call-update) | async-done | bytes 589840 | tf_op jit(solution)/shard_map/psum | solution.py:127
  355.5 1.3 fusion.97
  356.8 1.2 fusion.100
  358.0 50.4 %while.27 = (s32[]{:T(128)}, bf16[32,4608]{1,0:T(8,128)(2,1)S(1)}, bf16[8,32,4608]{2,1,0:T(8,128)(2,1)}, bf16[8,8,4608]{2,1,0:T(8,128)(2,1)}, bf16[8,4608]{1,0:T...) while((s32[]{:T(128)}, bf16[32,4608]{1,0:T(8,128)(2,1)S(1)}, ...), condition=%wide.region_13.14_spmd, body=%wide.region_10.13_spmd.sunk | while | flops 10036515 | bytes 3535725 | solution.py:133
  358.0 1.1 fusion.137
  360.1 1.2 fusion.138
  361.4 1.7 fusion.139
  363.1 1.2 fusion.140
  366.4 1.2 fusion.138
  367.7 1.7 fusion.139
  369.4 1.2 fusion.140
  372.7 1.2 fusion.138
  374.0 1.7 fusion.139
  375.7 1.2 fusion.140
  379.0 1.2 fusion.138
  380.3 1.7 fusion.139
  382.0 1.2 fusion.140
  385.3 1.2 fusion.138
  386.6 1.7 fusion.139
  388.3 1.2 fusion.140
  391.6 1.2 fusion.138
  392.9 1.7 fusion.139
  394.6 1.2 fusion.140
  397.9 1.2 fusion.138
  399.1 1.7 fusion.139
  400.9 1.2 fusion.140
  404.2 1.2 fusion.138
  405.4 1.7 fusion.139
  407.2 1.2 fusion.140
  408.4 4.6 %fusion.91 = bf16[256,4608]{1,0:T(8,128)(2,1)} fusion(f32[256,4608]{1,0:T(8,128)} %fusion.102, bf16[32,4608]{1,0:T(8,128)(2,1)S(1)} %get-tuple-element.159, s32[32]{0:T(128)S(1)} %sub.70), kind=kOutput, calls=%fused_computation.92 | convolution fusion | flops 79044608 | bytes 7372928 | tf_op jit(solution)/shard_map/dot_general | solution.py:138
  (104 shorter events, 35.8 us)
Async XLA Ops:
  7.2 23.5 %copy-start = (bf16[256,4608]{1,0:T(8,128)(2,1)S(1)}, bf16[256,4608]{1,0:T(8,128)(2,1)}, u32[]{:S(2)}) copy-start(bf16[256,4608]{1,0:T(8,128)(2,1)} %param.13) | copy-start | bytes 7077892
  7.2 24.9 %copy-start.4 = (bf16[4608]{0:T(1024)(128)(2,1)S(1)}, bf16[4608]{0:T(1024)(128)(2,1)}, u32[]{:S(2)}) copy-start(bf16[4608]{0:T(1024)(128)(2,1)} %param.17) | copy-start | bytes 27652
  7.2 24.9 %copy-start.3 = (bf16[2,1,4608]{2,0,1:T(2,128)(2,1)S(1)}, bf16[2,1,4608]{2,0,1:T(2,128)(2,1)}, u32[]{:S(2)}) copy-start(bf16[2,1,4608]{2,0,1:T(2,128)(2,1)} %param.14) | copy-start | bytes 55300
  7.2 30.8 %copy-start.1 = (bf16[2,1,8,4608]{3,2,1,0:T(8,128)(2,1)S(1)}, bf16[2,1,8,4608]{3,2,1,0:T(8,128)(2,1)}, u32[]{:S(2)}) copy-start(bf16[2,1,8,4608]{3,2,1,0:T(8,128)(2,1)} %param.15) | copy-start | bytes 442372
  7.2 39.0 %copy-start.2 = (bf16[2,1,8,4608]{3,2,1,0:T(8,128)(2,1)S(1)}, bf16[2,1,8,4608]{3,2,1,0:T(8,128)(2,1)}, u32[]{:S(2)}) copy-start(bf16[2,1,8,4608]{3,2,1,0:T(8,128)(2,1)} %param.16) | copy-start | bytes 442372
  7.2 147.8 %all-reduce.3.cloned.1.call-start = ((), (), s32[]{:S(2)}) async-start(), calls=%async_computation | async-start | bytes 589824 | tf_op jit(solution)/shard_map/psum | solution.py:94
  31.9 323.5 %all-reduce.5.cloned.1.call-start = ((), (), s32[]{:S(2)}) async-start(), calls=%async_computation.1 | async-start | bytes 1179648 | tf_op jit(solution)/shard_map/psum | solution.py:127
Sparse Core Ops, SparseCore 0:
  32.0 122.9 all-reduce.2
  228.3 127.1 all-reduce.4
where the time goes:
time: 422 us; the launch traced here: 420 us
  waiting for transfers between devices  224 us (53%)
  blocking collectives  85 us (20%)
  matrix products  47.9 us (11%)
  other arithmetic  40 us (9%)
  between operations  14.1 us (3%)
  local copies, waits for them, and re-layouts  7.85 us (2%)
    psum x1, waiting for transfers between devices, per_device(): head_in_grad = lax.psum(partial_value, ('section', 'dp'))  124 us
    psum x1, waiting for transfers between devices, per_device(): looked = lax.psum(looked, ('section', 'dp')).astype(jnp.float32)  101 us
    psum x1, blocking collectives, per_device(): lax.psum(jnp.stack([jnp.sum(powers, axis=1), jnp.sum(jnp.where(target_mas...  41.2 us
    all_gather x1, blocking collectives, per_device(): lax.all_gather(jnp.concatenate([token_ids, target_ids], 0), 'dp', axis=1,...  22.3 us
    dot_general x8, matrix products, layer_backward(): jnp.dot(preact_grad, first_proj, preferred_element_type=jnp.float32)  14 us
    dot_general x8, matrix products, layer_forward(): branch = jnp.dot(hidden, second_proj, preferred_element_type=jnp.float32)  12.8 us
    reduce_sum x17, other arithmetic, normalize(): scale = lax.rsqrt(jnp.mean(values * values, axis=-1, keepdims=True) + EPS)  10.7 us
    dot_general x8, matrix products, layer_backward(): lax.dot_general(activated, first_proj, (((1,), (1,)), ((), ())), preferre...  9.88 us
  transfers between devices with their start and end apart: 2, of which 2 were waited for; matrix products, arithmetic and copies ran while one was open for 1% of the time, Pallas kernels for 0%

commit v1 on v0

--- a/solution.py
+++ b/solution.py
@@ -91,7 +91,7 @@
         jnp.bfloat16
     )
     looked = jnp.dot(chosen, table, preferred_element_type=jnp.float32).astype(jnp.bfloat16)
-    looked = lax.psum(looked, ("section", "dp")).astype(jnp.float32)
+    looked = lax.psum(lax.psum(looked, "dp"), "section").astype(jnp.float32)
     rows = (looked * embed_scale).astype(jnp.bfloat16)
 
     def forward(rows, weights):

time: 422 us -> 400 us (0.948)
  waiting for transfers between devices: 224 us -> 204 us
    psum x1 -> x2, waiting for transfers between devices: 101 us -> 79.7 us  [per_device(): looked = lax.psum(lax.psum(looked, 'dp'), 'section').astype(jnp.float32)]
  transfers between devices with their start and end apart: 2 -> 3, of which waited for: 2 -> 3; matrix products, arithmetic and copies ran while one was open for 1% -> 1% of each run, Pallas kernels for 0% -> 0%
where the time goes in v1:
time: 400 us; the launch traced here: 397 us
  waiting for transfers between devices  204 us (51%)
  blocking collectives  82.9 us (21%)
  matrix products  47.9 us (12%)
  other arithmetic  40 us (10%)
  between operations  13.9 us (3%)
  local copies, waits for them, and re-layouts  7.85 us (2%)
    psum x1, waiting for transfers between devices, per_device(): head_in_grad = lax.psum(partial_value, ('section', 'dp'))  125 us
    psum x2, waiting for transfers between devices, per_device(): looked = lax.psum(lax.psum(looked, 'dp'), 'section').astype(jnp.float32)  79.7 us
    psum x1, blocking collectives, per_device(): lax.psum(jnp.stack([jnp.sum(powers, axis=1), jnp.sum(jnp.where(target_mas...  39.4 us
    all_gather x1, blocking collectives, per_device(): lax.all_gather(jnp.concatenate([token_ids, target_ids], 0), 'dp', axis=1,...  22.3 us
    dot_general x8, matrix products, layer_backward(): jnp.dot(preact_grad, first_proj, preferred_element_type=jnp.float32)  14 us
    dot_general x8, matrix products, layer_forward(): branch = jnp.dot(hidden, second_proj, preferred_element_type=jnp.float32)  12.8 us
    reduce_sum x17, other arithmetic, normalize(): scale = lax.rsqrt(jnp.mean(values * values, axis=-1, keepdims=True) + EPS)  10.7 us
    dot_general x8, matrix products, layer_backward(): lax.dot_general(activated, first_proj, (((1,), (1,)), ((), ())), preferre...  9.88 us
  transfers between devices with their start and end apart: 3, of which 3 were waited for; matrix products, arithmetic and copies ran while one was open for 1% of the time, Pallas kernels for 0%

profile of v1, /device:TPU:0, one launch (start us, length us, event | category | flops | bytes accessed | tf_op | source)
XLA Modules:
  0.0 397.4 jit_solution(5556878007330996495)
XLA Ops:
  8.2 22.3 %all-gather = s32[8,2,4]{2,1,0:T(2,128)S(1)} all-gather(s32[1,2,4]{2,1,0:T(2,128)S(1)} %bitcast.102), channel_id=1, replica_groups=mesh['section'=4,'dp'=8] {'dp'}, dimensions={0}, use_global_device_ids=true | all-gather | bytes 288 | tf_op jit(solution)/shard_map/all_gather | solution.py:83
  30.6 1.2 convolution_convert_fusion
  32.1 5.3 %all_gather.13 = bf16[2,4,4608]{2,0,1:T(2,128)(2,1)S(1)} all-gather(bf16[2,1,4608]{2,0,1:T(2,128)(2,1)S(1)} %copy-done.3), channel_id=1, replica_groups=mesh['section'=4,'dp'=8] {'section'}, dimensions={1}, use_global_device_ids=true | all-gather | bytes 92160 | tf_op jit(solution)/shard_map/all_gather | solution.py:84
  38.0 8.1 %all_gather.14 = bf16[2,4,8,4608]{3,2,1,0:T(8,128)(2,1)} all-gather(bf16[2,1,8,4608]{3,2,1,0:T(8,128)(2,1)S(1)} %copy-done.1), channel_id=1, replica_groups=mesh['section'=4,'dp'=8] {'section'}, dimensions={1}, use_global_device_ids=true | all-gather | bytes 737280 | tf_op jit(solution)/shard_map/all_gather | solution.py:85
  46.1 54.1 %all-reduce.4.cloned.1.call-done = bf16[32,4608]{1,0:T(8,128)(2,1)} async-done(((bf16[32,4608]{1,0:T(8,128)(2,1)}), bf16[32,4608]{1,0:T(8,128)(2,1)}) %all-reduce.4.cloned.1.call-update) | async-done | bytes 294928 | tf_op jit(solution)/shard_map/psum | solution.py:94
  100.2 8.0 %all_gather.15 = bf16[2,4,8,4608]{3,2,1,0:T(8,128)(2,1)} all-gather(bf16[2,1,8,4608]{3,2,1,0:T(8,128)(2,1)S(1)} %copy-done.2), channel_id=1, replica_groups=mesh['section'=4,'dp'=8] {'section'}, dimensions={1}, use_global_device_ids=true | all-gather | bytes 737280 | tf_op jit(solution)/shard_map/all_gather | solution.py:86
  108.2 25.7 %all-reduce.6.cloned.1.call-done = bf16[32,4608]{1,0:T(8,128)(2,1)} async-done(((bf16[32,4608]{1,0:T(8,128)(2,1)}), bf16[32,4608]{1,0:T(8,128)(2,1)}) %all-reduce.6.cloned.1.call-update) | async-done | bytes 294928 | tf_op jit(solution)/shard_map/psum | solution.py:94
  134.9 28.2 %while.26 = (s32[]{:T(128)}, bf16[32,4608]{1,0:T(8,128)(2,1)S(1)}, bf16[8,32,4608]{2,1,0:T(8,128)(2,1)}, bf16[8,4608]{1,0:T(8,128)(2,1)}, bf16[8,8,4608]{2,1,0:T...) while((s32[]{:T(128)}, bf16[32,4608]{1,0:T(8,128)(2,1)S(1)}, bf16[8,32,4608]{2,1,0:T(8,128)(2,1)}, ...), condition=%wide.region_4.5_spmd, body=%wide.region_2.4_spmd.sunk | while | flops 6200098 | bytes 2556893 | solution.py:100
  136.8 1.6 fusion.132
  140.4 1.6 fusion.132
  143.9 1.6 fusion.132
  147.4 1.6 fusion.132
  151.0 1.6 fusion.132
  154.5 1.6 fusion.132
  158.0 1.6 fusion.132
  161.6 1.6 fusion.132
  164.3 39.4 %psum.30 = f32[2,32]{1,0:T(2,128)S(1)} all-reduce(f32[2,32]{1,0:T(2,128)S(1)} %pad_maximum_fusion), channel_id=1, replica_groups=mesh['section'=4,'dp'=8] {'section','dp'}, use_global_device_ids=true, to_apply=%region_8.9 | all-reduce | flops 64 | bytes 512 | tf_op jit(solution)/shard_map/psum | solution.py:111
  203.8 1.4 fusion.107
  205.8 3.0 fusion.102
  208.8 124.5 %all-reduce.8.cloned.1.call-done = f32[32,4608]{1,0:T(8,128)} async-done(((f32[32,4608]{1,0:T(8,128)}), f32[32,4608]{1,0:T(8,128)}) %all-reduce.8.cloned.1.call-update) | async-done | bytes 589840 | tf_op jit(solution)/shard_map/psum | solution.py:127
  333.4 1.3 fusion.97
  334.7 1.2 fusion.100
  335.9 50.3 %while.27 = (s32[]{:T(128)}, bf16[32,4608]{1,0:T(8,128)(2,1)S(1)}, bf16[8,32,4608]{2,1,0:T(8,128)(2,1)}, bf16[8,8,4608]{2,1,0:T(8,128)(2,1)}, bf16[8,4608]{1,0:T...) while((s32[]{:T(128)}, bf16[32,4608]{1,0:T(8,128)(2,1)S(1)}, ...), condition=%wide.region_14.15_spmd, body=%wide.region_11.14_spmd.sunk | while | flops 10036515 | bytes 3535725 | solution.py:133
  338.0 1.2 fusion.138
  339.3 1.7 fusion.139
  341.0 1.2 fusion.140
  344.3 1.2 fusion.138
  345.6 1.7 fusion.139
  347.3 1.2 fusion.140
  350.6 1.2 fusion.138
  351.9 1.7 fusion.139
  353.6 1.2 fusion.140
  356.9 1.2 fusion.138
  358.2 1.7 fusion.139
  359.9 1.2 fusion.140
  363.2 1.2 fusion.138
  364.5 1.7 fusion.139
  366.2 1.2 fusion.140
  369.5 1.2 fusion.138
  370.7 1.7 fusion.139
  372.5 1.2 fusion.140
  375.8 1.2 fusion.138
  377.0 1.7 fusion.139
  378.8 1.2 fusion.140
  382.1 1.2 fusion.138
  383.3 1.7 fusion.139
  385.1 1.2 fusion.140
  386.3 4.6 %fusion.91 = bf16[256,4608]{1,0:T(8,128)(2,1)} fusion(f32[256,4608]{1,0:T(8,128)} %fusion.102, bf16[32,4608]{1,0:T(8,128)(2,1)S(1)} %get-tuple-element.159, s32[32]{0:T(128)S(1)} %sub.70), kind=kOutput, calls=%fused_computation.92 | convolution fusion | flops 79044608 | bytes 7372928 | tf_op jit(solution)/shard_map/dot_general | solution.py:138
  (107 shorter events, 37.0 us)
Async XLA Ops:
  7.2 23.5 %copy-start = (bf16[256,4608]{1,0:T(8,128)(2,1)S(1)}, bf16[256,4608]{1,0:T(8,128)(2,1)}, u32[]{:S(2)}) copy-start(bf16[256,4608]{1,0:T(8,128)(2,1)} %param.13) | copy-start | bytes 7077892
  7.2 24.9 %copy-start.4 = (bf16[4608]{0:T(1024)(128)(2,1)S(1)}, bf16[4608]{0:T(1024)(128)(2,1)}, u32[]{:S(2)}) copy-start(bf16[4608]{0:T(1024)(128)(2,1)} %param.17) | copy-start | bytes 27652
  7.2 24.9 %copy-start.3 = (bf16[2,1,4608]{2,0,1:T(2,128)(2,1)S(1)}, bf16[2,1,4608]{2,0,1:T(2,128)(2,1)}, u32[]{:S(2)}) copy-start(bf16[2,1,4608]{2,0,1:T(2,128)(2,1)} %param.14) | copy-start | bytes 55300
  7.2 30.8 %copy-start.1 = (bf16[2,1,8,4608]{3,2,1,0:T(8,128)(2,1)S(1)}, bf16[2,1,8,4608]{3,2,1,0:T(8,128)(2,1)}, u32[]{:S(2)}) copy-start(bf16[2,1,8,4608]{3,2,1,0:T(8,128)(2,1)} %param.15) | copy-start | bytes 442372
  7.2 93.0 %copy-start.2 = (bf16[2,1,8,4608]{3,2,1,0:T(8,128)(2,1)S(1)}, bf16[2,1,8,4608]{3,2,1,0:T(8,128)(2,1)}, u32[]{:S(2)}) copy-start(bf16[2,1,8,4608]{3,2,1,0:T(8,128)(2,1)} %param.16) | copy-start | bytes 442372
  7.2 92.9 %all-reduce.4.cloned.1.call-start = ((), (), s32[]{:S(2)}) async-start(), calls=%async_computation | async-start | bytes 589824 | tf_op jit(solution)/shard_map/psum | solution.py:94
  31.9 102.0 %all-reduce.6.cloned.1.call-start = ((), (), s32[]{:S(2)}) async-start(), calls=%async_computation.1 | async-start | bytes 589824 | tf_op jit(solution)/shard_map/psum | solution.py:94
  100.2 233.2 %all-reduce.8.cloned.1.call-start = ((), (), s32[]{:S(2)}) async-start(), calls=%async_computation.2 | async-start | bytes 1179648 | tf_op jit(solution)/shard_map/psum | solution.py:127
Sparse Core Ops, SparseCore 0:
  32.0 68.0 all-reduce.3
  102.6 31.2 all-reduce.5
  205.3 127.9 all-reduce.7
